TPU v7x, 32 devices: a whole 2x2x4 slice. The times are simulated.
32 devices in a mesh: dp: 4 (over x, core), ctx: 8 (over z, y).
Axes of the slice: x: 2, y: 2, z: 4, core: 2. Of those that a mesh axis runs over, the one named last changes fastest.
Arguments:
- queries: bfloat16 [4, 2048, 1024], P('dp', 'ctx'), may hold values from -4.5 to 4.5
- keys: bfloat16 [4, 2048, 1024], P('dp', 'ctx'), may hold values from -4.5 to 4.5
- values: bfloat16 [4, 2048, 1024], P('dp', 'ctx'), may hold values from -6 to 6
- out_grad: bfloat16 [4, 2048, 2048], P('dp', 'ctx'), may hold values from -6 to 6
- chosen: int32 [4, 8], P('dp'), may hold values from -1 to 15, as said below
- proj: bfloat16 [1024, 2048], P('ctx', 'dp'), may hold values from -0.1875 to 0.1875
Outputs:
- attn_out: bfloat16 [4, 2048, 2048], P('dp', 'ctx')
- q_grad: bfloat16 [4, 2048, 1024], P('dp', 'ctx')
- k_grad: bfloat16 [4, 2048, 1024], P('dp', 'ctx')
- v_grad: bfloat16 [4, 2048, 1024], P('dp', 'ctx')
- proj_grad: float32 [1024, 2048], P('ctx', 'dp')
Inputs may be any that keep to these rules, and one draw needn't show every extreme that they name: chosen[d, c] is -1 or the index pos // 128 of one of the blocks that ctx index c stores (position spans c and 15 - c, of 1 block each); every sequence has one or more entries that are not -1.
All inputs are finite; a program needn't handle non-finite values.
Results may differ from a plain program's by a relative error of at most 0.023.
Values may be sent and summed in bfloat16 or wider, within the bound.
A program may use at most 192 MiB of HBM per device.

v0:
```python
import math

import jax
import jax.numpy as jnp
from jax import lax
from jax.sharding import PartitionSpec as P

BLOCK = 128


def cross_dot(left_op, right_op):
    return lax.dot_general(
        left_op, right_op, (((1,), (1,)), ((), ())), preferred_element_type=jnp.float32
    )


def inner_dot(left_op, right_op):
    return lax.dot_general(
        left_op, right_op, (((0,), (0,)), ((), ())), preferred_element_type=jnp.float32
    )


def head_probs(
    query_block,
    query_pos,
    query_live,
    query_ids,
    heads_k,
    slot_pos,
    slot_live,
    slot_ids,
    score_scale,
):
    scores = cross_dot(query_block, heads_k) * score_scale
    allowed = query_live[:, None] & slot_live[None, :] & (
        slot_pos[None, :] <= query_pos[:, None]
    ) | (query_ids[:, None] == slot_ids[None, :])
    masked = jnp.where(allowed, scores, -1e30)
    row_max = jnp.max(masked, axis=1, keepdims=True)
    exp_terms = jnp.where(allowed, jnp.exp(masked - row_max), 0.0)
    return exp_terms / jnp.sum(exp_terms, axis=1, keepdims=True)


def shards(queries, keys, values, out_grad, chosen, proj):
    ctx_count = lax.axis_size("ctx")
    ctx_index = lax.axis_index("ctx")
    tokens = queries.shape[1]
    half_rows = tokens // 2
    block_rows = BLOCK
    picked = chosen[0]
    own_pick = lax.dynamic_index_in_dim(picked, ctx_index, 0, keepdims=False)
    own_live = own_pick >= 0
    first_pos = jnp.where(own_live, own_pick, 0) * block_rows
    local_row = jnp.where(
        first_pos // half_rows == ctx_index,
        first_pos % half_rows,
        half_rows + first_pos % half_rows,
    )
    row_start = jnp.where(own_live, local_row, 0)

    def take_rows(source):
        slot_block = lax.dynamic_slice_in_dim(source[0], row_start, block_rows, 0)
        return jnp.where(own_live, slot_block, jnp.zeros((), source.dtype))

    def place_rows(slot_block, template):
        return lax.dynamic_update_slice_in_dim(
            jnp.zeros(template.shape, jnp.bfloat16), slot_block[None], row_start, 1
        )

    q_slot = take_rows(queries)
    k_slot = take_rows(keys)
    v_slot = take_rows(values)
    g_slot = take_rows(out_grad)
    heads_q, heads_k, heads_v = (
        lax.all_to_all(q_slot, "ctx", split_axis=1, concat_axis=0, tiled=True),
        lax.all_to_all(k_slot, "ctx", split_axis=1, concat_axis=0, tiled=True),
        lax.all_to_all(v_slot, "ctx", split_axis=1, concat_axis=0, tiled=True),
    )
    slot_count = ctx_count * block_rows
    offsets = jnp.arange(block_rows, dtype=jnp.int32)
    safe_pick = jnp.where(picked >= 0, picked, 0)
    slot_pos = (safe_pick[:, None] * block_rows + offsets[None, :]).reshape(slot_count)
    slot_live = jnp.repeat(picked >= 0, block_rows)
    slot_ids = jnp.arange(slot_count, dtype=jnp.int32)
    head_dim = heads_q.shape[1]
    score_scale = 1.0 / math.sqrt(head_dim)
    step_rows = min(512, slot_count)
    step_count = slot_count // step_rows
    attn_parts = []
    prob_store = []
    prob_b_store = []
    for step_index in range(step_count):
        row_low = step_index * step_rows
        window = slice(row_low, row_low + step_rows)
        attn_prob = head_probs(
            heads_q[window],
            slot_pos[window],
            slot_live[window],
            slot_ids[window],
            heads_k,
            slot_pos,
            slot_live,
            slot_ids,
            score_scale,
        )
        prob_b = attn_prob.astype(jnp.bfloat16)
        prob_store.append(attn_prob)
        prob_b_store.append(prob_b)
        attn_parts.append(
            jnp.dot(prob_b, heads_v, preferred_element_type=jnp.float32).astype(jnp.bfloat16)
        )
    attn_heads = jnp.concatenate(attn_parts, 0)
    attn_local = lax.all_to_all(attn_heads, "ctx", split_axis=0, concat_axis=1, tiled=True)
    head_rows = lax.all_gather(proj, "dp", axis=1, tiled=True)
    full_proj = lax.all_gather(head_rows, "ctx", axis=0, tiled=True)
    mixed = jnp.dot(attn_local, full_proj, preferred_element_type=jnp.float32).astype(jnp.bfloat16)
    attn_out = place_rows(mixed, out_grad)
    part_rows = lax.all_gather(g_slot, "ctx", axis=0, tiled=True)
    weight_term = inner_dot(attn_heads, part_rows)
    rows_grad = cross_dot(part_rows, head_rows)
    weight_term, rows_grad = (weight_term, rows_grad)
    attn_grad = rows_grad.astype(jnp.bfloat16)
    proj_grad = lax.psum_scatter(weight_term, "dp", scatter_dimension=1, tiled=True)
    key_grad = jnp.zeros((slot_count, head_dim), jnp.float32)
    value_grad = jnp.zeros((slot_count, head_dim), jnp.float32)
    query_parts = []
    for step_index in range(step_count):
        row_low = step_index * step_rows
        window = slice(row_low, row_low + step_rows)
        attn_prob = prob_store[step_index]
        prob_b = prob_b_store[step_index]
        grad_block = attn_grad[window]
        row_delta = jnp.sum(
            grad_block.astype(jnp.float32) * attn_heads[window].astype(jnp.float32),
            axis=1,
            keepdims=True,
        )
        score_grad = (attn_prob * (cross_dot(grad_block, heads_v) - row_delta)).astype(jnp.bfloat16)
        query_parts.append(
            (jnp.dot(score_grad, heads_k, preferred_element_type=jnp.float32) * score_scale).astype(
                jnp.bfloat16
            )
        )
        key_grad = key_grad + inner_dot(score_grad, heads_q[window])
        value_grad = value_grad + inner_dot(prob_b, grad_block)
    q_heads_grad = jnp.concatenate(query_parts, 0)
    k_heads_grad = (key_grad * score_scale).astype(jnp.bfloat16)
    v_heads_grad = value_grad.astype(jnp.bfloat16)
    q_back, k_back, v_back = (
        lax.all_to_all(q_heads_grad, "ctx", split_axis=0, concat_axis=1, tiled=True),
        lax.all_to_all(k_heads_grad, "ctx", split_axis=0, concat_axis=1, tiled=True),
        lax.all_to_all(v_heads_grad, "ctx", split_axis=0, concat_axis=1, tiled=True),
    )
    return (
        attn_out,
        place_rows(q_back, queries),
        place_rows(k_back, keys),
        place_rows(v_back, values),
        proj_grad,
    )


def solution(mesh):
    placed = (
        P("dp", "ctx", None),
        P("dp", "ctx", None),
        P("dp", "ctx", None),
        P("dp", "ctx", None),
        P("dp", None),
        P("ctx", "dp"),
    )
    return jax.shard_map(
        shards,
        mesh=mesh,
        in_specs=placed,
        out_specs=(
            P("dp", "ctx", None),
            P("dp", "ctx", None),
            P("dp", "ctx", None),
            P("dp", "ctx", None),
            P("ctx", "dp"),
        ),
        check_vma=False,
    )
```

profile of v0, /device:TPU:0, one launch (start us, length us, event | category | flops | bytes accessed | tf_op | source)
XLA Modules:
  0.0 224.0 jit_solution(12597363358342801564)
XLA Ops:
  9.9 2.0 dynamic-slice_select_fusion
  12.0 10.2 %all_gather.9 = bf16[128,2048]{1,0:T(8,128)(2,1)} all-gather(bf16[128,512]{1,0:T(8,128)(2,1)} %param.11), channel_id=1, replica_groups=mesh['dp'=4,'ctx'=8] {'dp'}, dimensions={1}, use_global_device_ids=true | all-gather | bytes 655360 | tf_op jit(solution)/shard_map/all_gather | solution.py:114
  23.4 5.8 %all-to-all-start.1 = ((bf16[128,8,128]{0,2,1:T(8,128)(2,1)}), bf16[128,8,128]{0,2,1:T(8,128)(2,1)S(1)}, u32[]{:S(2)}, u32[]{:S(2)}) async-start(bf16[128,8,128]{0,2,1:T(8,128)(2,1)} %bitcast.9), calls=%async_computation.1 | async-start | bytes 524288 | tf_op jit(solution)/shard_map/all_to_all | solution.py:76
  30.6 15.6 %all-to-all-done.1 = bf16[128,8,128]{0,2,1:T(8,128)(2,1)S(1)} async-done(((bf16[128,8,128]{0,2,1:T(8,128)(2,1)}), bf16[128,8,128]{0,2,1:T(8,128)(2,1)S(1)}, u32[]{:S(2)}, u32[]{:S(2)}) %all-to-all-start.1) | async-done | bytes 262176 | tf_op jit(solution)/shard_map/all_to_all | solution.py:76
  46.3 3.5 %all-to-all-start = ((bf16[128,8,128]{0,2,1:T(8,128)(2,1)}), bf16[128,8,128]{0,2,1:T(8,128)(2,1)S(1)}, u32[]{:S(2)}, u32[]{:S(2)}) async-start(bf16[128,8,128]{0,2,1:T(8,128)(2,1)} %bitcast.6), calls=%async_computation | async-start | bytes 524288 | tf_op jit(solution)/shard_map/all_to_all | solution.py:75
  50.5 12.3 %all-to-all-done = bf16[128,8,128]{0,2,1:T(8,128)(2,1)S(1)} async-done(((bf16[128,8,128]{0,2,1:T(8,128)(2,1)}), bf16[128,8,128]{0,2,1:T(8,128)(2,1)S(1)}, u32[]{:S(2)}, u32[]{:S(2)}) %all-to-all-start) | async-done | bytes 262176 | tf_op jit(solution)/shard_map/all_to_all | solution.py:75
  62.8 5.5 %all-to-all-start.2 = ((bf16[128,8,128]{0,2,1:T(8,128)(2,1)}), bf16[128,8,128]{0,2,1:T(8,128)(2,1)S(1)}, u32[]{:S(2)}, u32[]{:S(2)}) async-start(bf16[128,8,128]{0,2,1:T(8,128)(2,1)} %bitcast.12), calls=%async_computation.2 | async-start | bytes 524288 | tf_op jit(solution)/shard_map/all_to_all | solution.py:77
  68.9 15.9 %all-to-all-done.2 = bf16[128,8,128]{0,2,1:T(8,128)(2,1)S(1)} async-done(((bf16[128,8,128]{0,2,1:T(8,128)(2,1)}), bf16[128,8,128]{0,2,1:T(8,128)(2,1)S(1)}, u32[]{:S(2)}, u32[]{:S(2)}) %all-to-all-start.2) | async-done | bytes 262176 | tf_op jit(solution)/shard_map/all_to_all | solution.py:77
  87.3 3.0 %fusion.11 = (f32[512]{0:T(512)S(1)}, f32[512]{0:T(512)S(1)}) fusion(f32[512,1024]{1,0:T(8,128)S(1)} %get-tuple-element.21, f32[512]{0:T(512)S(1)} %get-tuple-element.9, s32[512]{0:T(512)S(1)} %slice.46, s32[512]{0:T(512)S(1)} %get-tuple-element.16, s32[1024]{0:T(1024)S(1)} %get-tuple-element.19, pred[1024]{0:T(1024)(128)(4,1)S(1)} %broadcast_bitcast_fusion, ...), kind=kLoop, calls=%fused_computation.22 | loop fusion | flops 10484736 | bytes 4216832 | tf_op jit(solution)/shard_map/reduce_sum | solution.py:41
  90.3 3.8 %fusion.10 = (f32[512,1024]{1,0:T(8,128)}, f32[512,1024]{1,0:T(8,128)S(1)}) fusion(f32[512,1024]{1,0:T(8,128)S(1)} %get-tuple-element.21, f32[512]{0:T(512)S(1)} %get-tuple-element.7, f32[512]{0:T(512)S(1)} %get-tuple-element.9, s32[512]{0:T(512)S(1)} %slice.46, s32[512]{0:T(512)S(1)} %get-tuple-element.16, s32[1024]{0:T(1024)S(1)} %get-tuple-element.19, ...), kind=kLoop, calls=%fused_computation.21 | loop fusion | flops 10485760 | bytes 8411136 | tf_op jit(solution)/shard_map/div | solution.py:41
  94.6 4.0 %all-gather.6.cloned.1.call-done = bf16[1,1024,2048]{2,1,0:T(8,128)(2,1)} async-done(((bf16[1,128,2048]{2,1,0:T(8,128)(2,1)}), bf16[1,1024,2048]{2,1,0:T(8,128)(2,1)}) %all-gather.6.cloned.1.call-update) | async-done | bytes 4194320 | tf_op jit(solution)/shard_map/all_gather | solution.py:118
  98.6 3.7 %fusion.16 = bf16[1024,128]{1,0:T(8,128)(2,1)S(1)} fusion(bf16[128,2048]{1,0:T(8,128)(2,1)} %all_gather.9, bf16[1,1024,2048]{2,1,0:T(8,128)(2,1)} %all-gather.6.cloned.1.call-done), kind=kOutput, calls=%fused_computation.27 | convolution fusion | flops 537001984 | bytes 4980736 | tf_op jit(solution)/shard_map/dot_general | solution.py:12
  104.0 4.0 %all-to-all-start.6 = ((bf16[8,128,128]{2,1,0:T(8,128)(2,1)}), bf16[8,128,128]{2,1,0:T(8,128)(2,1)}, u32[]{:S(2)}, u32[]{:S(2)}) async-start(bf16[8,128,128]{2,1,0:T(8,128)(2,1)} %bitcast.79), calls=%async_computation.6 | async-start | bytes 524288 | tf_op jit(solution)/shard_map/all_to_all | solution.py:152
  108.1 2.3 %multiply_reduce_fusion.1 = (f32[512]{0:T(512)S(1)}, f32[512]{0:T(512)S(1)}, bf16[512,128]{1,0:T(8,128)(2,1)S(1)}) fusion(bf16[1024,128]{1,0:T(8,128)(2,1)S(1)} %fusion.16, bf16[512,128]{1,0:T(8,128)(2,1)S(1)} %convolution_convert_fusion.1, bf16[1024,128]{1,0:T(8,128)(2,1)S(1)} %bitcast.69, f32[512,1024]{1,0:T(8,128)} %get-tuple-element.13), kind=kOutput, calls=%fused_computation.43 | convolution fusion | flops 135330816 | bytes 2887680 | tf_op jit(solution)/shard_map/dot_general | solution.py:110
  117.6 7.5 %all-to-all-done.6 = bf16[8,128,128]{2,1,0:T(8,128)(2,1)} async-done(((bf16[8,128,128]{2,1,0:T(8,128)(2,1)}), bf16[8,128,128]{2,1,0:T(8,128)(2,1)}, u32[]{:S(2)}, u32[]{:S(2)}) %all-to-all-start.6) | async-done | bytes 262176 | tf_op jit(solution)/shard_map/all_to_all | solution.py:152
  125.1 3.6 %all-to-all-start.5 = ((bf16[8,128,128]{2,1,0:T(8,128)(2,1)}), bf16[8,128,128]{2,1,0:T(8,128)(2,1)S(1)}, u32[]{:S(2)}, u32[]{:S(2)}) async-start(bf16[8,128,128]{2,1,0:T(8,128)(2,1)} %bitcast.25), calls=%async_computation.5 | async-start | bytes 524288 | tf_op jit(solution)/shard_map/all_to_all | solution.py:151
  130.3 8.7 %all-to-all-done.5 = bf16[8,128,128]{2,1,0:T(8,128)(2,1)S(1)} async-done(((bf16[8,128,128]{2,1,0:T(8,128)(2,1)}), bf16[8,128,128]{2,1,0:T(8,128)(2,1)S(1)}, u32[]{:S(2)}, u32[]{:S(2)}) %all-to-all-start.5) | async-done | bytes 262176 | tf_op jit(solution)/shard_map/all_to_all | solution.py:151
  139.0 3.5 %all-to-all-start.4 = ((bf16[8,128,128]{2,1,0:T(8,128)(2,1)}), bf16[8,128,128]{2,1,0:T(8,128)(2,1)S(1)}, u32[]{:S(2)}, u32[]{:S(2)}) async-start(bf16[8,128,128]{2,1,0:T(8,128)(2,1)} %bitcast.23), calls=%async_computation.4 | async-start | bytes 524288 | tf_op jit(solution)/shard_map/all_to_all | solution.py:150
  143.3 15.6 %all-to-all-done.4 = bf16[8,128,128]{2,1,0:T(8,128)(2,1)S(1)} async-done(((bf16[8,128,128]{2,1,0:T(8,128)(2,1)}), bf16[8,128,128]{2,1,0:T(8,128)(2,1)S(1)}, u32[]{:S(2)}, u32[]{:S(2)}) %all-to-all-start.4) | async-done | bytes 262176 | tf_op jit(solution)/shard_map/all_to_all | solution.py:150
  159.0 3.7 %all-to-all-start.3 = ((bf16[8,128,128]{1,2,0:T(8,128)(2,1)}), bf16[8,128,128]{1,2,0:T(8,128)(2,1)S(1)}, u32[]{:S(2)}, u32[]{:S(2)}) async-start(bf16[8,128,128]{1,2,0:T(8,128)(2,1)} %copy.27), calls=%async_computation.3 | async-start | bytes 524288 | tf_op jit(solution)/shard_map/all_to_all | solution.py:113
  170.1 20.4 %all-gather.4.cloned.1.call-done = bf16[1024,2048]{1,0:T(8,128)(2,1)} async-done(((bf16[128,2048]{1,0:T(8,128)(2,1)}), bf16[1024,2048]{1,0:T(8,128)(2,1)}) %all-gather.4.cloned.1.call-update) | async-done | bytes 4194320 | tf_op jit(solution)/shard_map/all_gather | solution.py:115
  190.5 2.9 %fusion.4 = bf16[1,128,2048]{2,1,0:T(8,128)(2,1)S(1)} fusion(bf16[128,1024]{0,1:T(8,128)(2,1)S(1)} %bitcast.78, bf16[1024,2048]{1,0:T(8,128)(2,1)} %all-gather.4.cloned.1.call-done), kind=kOutput, calls=%fused_computation.5 | convolution fusion | flops 537133056 | bytes 4980736 | tf_op jit(solution)/shard_map/dot_general | solution.py:116
  193.6 2.9 %dynamic_update_slice.12 = bf16[1,256,2048]{2,1,0:T(8,128)(2,1)S(1)} dynamic-update-slice(bf16[1,256,2048]{2,1,0:T(8,128)(2,1)S(1)} %broadcast_in_dim.59, bf16[1,128,2048]{2,1,0:T(8,128)(2,1)S(1)} %fusion.4, s32[]{:T(128)} %constant.48.clone.1, s32[]{:T(128)S(6)} %select_n.105, s32[]{:T(128)} %constant.48.clone.1) | dynamic-update-slice | bytes 1048580 | tf_op jit(solution)/shard_map/dynamic_update_slice | solution.py:66
  196.5 20.9 %reduce-scatter.2.cloned.1.call-done = f32[128,512]{1,0:T(8,128)} async-done(((f32[128,2048]{1,0:T(8,128)}), f32[128,512]{1,0:T(8,128)}) %reduce-scatter.2.cloned.1.call-update) | async-done | bytes 262160 | tf_op jit(solution)/shard_map/reduce_scatter | solution.py:123
  (98 shorter events, 26.9 us)
Async XLA Ops:
  7.2 22.0 %copy-start = (bf16[1,256,1024]{2,1,0:T(8,128)(2,1)S(1)}, bf16[1,256,1024]{2,1,0:T(8,128)(2,1)}, u32[]{:S(2)}) copy-start(bf16[1,256,1024]{2,1,0:T(8,128)(2,1)} %param.6) | copy-start | bytes 1572868
  7.2 15.1 %copy-start.17 = (bf16[1,256,1024]{2,1,0:T(8,128)(2,1)S(1)}, bf16[1,256,1024]{2,1,0:T(8,128)(2,1)}, u32[]{:S(2)}) copy-start(bf16[1,256,1024]{2,1,0:T(8,128)(2,1)} %param.7) | copy-start | bytes 1572868
  7.2 15.1 %copy-start.16 = (bf16[1,256,1024]{2,1,0:T(8,128)(2,1)S(1)}, bf16[1,256,1024]{2,1,0:T(8,128)(2,1)}, u32[]{:S(2)}) copy-start(bf16[1,256,1024]{2,1,0:T(8,128)(2,1)} %param.8) | copy-start | bytes 1572868
  7.2 91.4 %all-gather.6.cloned.1.call-start = ((), (), s32[]{:S(2)}) async-start(), calls=%async_computation.10 | async-start | bytes 4718592 | tf_op jit(solution)/shard_map/all_gather | solution.py:118
  12.0 178.6 %all-gather.4.cloned.1.call-start = ((), (), s32[]{:S(2)}) async-start(), calls=%async_computation.8 | async-start | bytes 4718592 | tf_op jit(solution)/shard_map/all_gather | solution.py:115
  22.3 7.4 %copy-start.18 = (s32[1,8]{1,0:T(1,128)S(1)}, s32[1,8]{1,0:T(1,128)}, u32[]{:S(2)}) copy-start(s32[1,8]{1,0:T(1,128)} %param.10) | copy-start | bytes 100
  23.4 22.9 %all-to-all-start.1 = ((bf16[128,8,128]{0,2,1:T(8,128)(2,1)}), bf16[128,8,128]{0,2,1:T(8,128)(2,1)S(1)}, u32[]{:S(2)}, u32[]{:S(2)}) async-start(bf16[128,8,128]{0,2,1:T(8,128)(2,1)} %bitcast.9), calls=%async_computation.1 | async-start | bytes 524288 | tf_op jit(solution)/shard_map/all_to_all | solution.py:76
  46.3 16.5 %all-to-all-start = ((bf16[128,8,128]{0,2,1:T(8,128)(2,1)}), bf16[128,8,128]{0,2,1:T(8,128)(2,1)S(1)}, u32[]{:S(2)}, u32[]{:S(2)}) async-start(bf16[128,8,128]{0,2,1:T(8,128)(2,1)} %bitcast.6), calls=%async_computation | async-start | bytes 524288 | tf_op jit(solution)/shard_map/all_to_all | solution.py:75
  62.8 22.0 %all-to-all-start.2 = ((bf16[128,8,128]{0,2,1:T(8,128)(2,1)}), bf16[128,8,128]{0,2,1:T(8,128)(2,1)S(1)}, u32[]{:S(2)}, u32[]{:S(2)}) async-start(bf16[128,8,128]{0,2,1:T(8,128)(2,1)} %bitcast.12), calls=%async_computation.2 | async-start | bytes 524288 | tf_op jit(solution)/shard_map/all_to_all | solution.py:77
  68.7 18.6 %copy-start.6 = (bf16[4,128,128]{2,1,0:T(8,128)(2,1)}, bf16[4,128,128]{2,1,0:T(8,128)(2,1)S(1)}, u32[]{:S(2)}) copy-start(bf16[4,128,128]{2,1,0:T(8,128)(2,1)S(1)} %copy.26) | copy-start | bytes 393220
  68.9 18.4 %copy-start.14 = (bf16[4,128,128]{2,1,0:T(8,128)(2,1)}, bf16[4,128,128]{2,1,0:T(8,128)(2,1)S(1)}, u32[]{:S(2)}) copy-start(bf16[4,128,128]{2,1,0:T(8,128)(2,1)S(1)} %copy.21) | copy-start | bytes 393220
  98.6 3.7 %copy-start.1 = (f32[512,1024]{1,0:T(8,128)S(1)}, f32[512,1024]{1,0:T(8,128)}, u32[]{:S(2)}) copy-start(f32[512,1024]{1,0:T(8,128)} %get-tuple-element.13) | copy-start | bytes 6291460
  104.0 21.0 %all-to-all-start.6 = ((bf16[8,128,128]{2,1,0:T(8,128)(2,1)}), bf16[8,128,128]{2,1,0:T(8,128)(2,1)}, u32[]{:S(2)}, u32[]{:S(2)}) async-start(bf16[8,128,128]{2,1,0:T(8,128)(2,1)} %bitcast.79), calls=%async_computation.6 | async-start | bytes 524288 | tf_op jit(solution)/shard_map/all_to_all | solution.py:152
  108.1 109.4 %reduce-scatter.2.cloned.1.call-start = ((), (), s32[]{:S(2)}) async-start(), calls=%async_computation.9 | async-start | bytes 1310720 | tf_op jit(solution)/shard_map/reduce_scatter | solution.py:123
  110.4 2.9 %copy-start.8 = (bf16[512,128]{1,0:T(8,128)(2,1)}, bf16[512,128]{1,0:T(8,128)(2,1)S(1)}, u32[]{:S(2)}) copy-start(bf16[512,128]{1,0:T(8,128)(2,1)S(1)} %get-tuple-element.22) | copy-start | bytes 393220
  110.4 2.9 %copy-start.5 = (bf16[1,1024,2048]{2,1,0:T(8,128)(2,1)S(1)}, bf16[1,1024,2048]{2,1,0:T(8,128)(2,1)}, u32[]{:S(2)}) copy-start(bf16[1,1024,2048]{2,1,0:T(8,128)(2,1)} %all-gather.6.cloned.1.call-done) | copy-start | bytes 12582916
  125.1 13.9 %all-to-all-start.5 = ((bf16[8,128,128]{2,1,0:T(8,128)(2,1)}), bf16[8,128,128]{2,1,0:T(8,128)(2,1)S(1)}, u32[]{:S(2)}, u32[]{:S(2)}) async-start(bf16[8,128,128]{2,1,0:T(8,128)(2,1)} %bitcast.25), calls=%async_computation.5 | async-start | bytes 524288 | tf_op jit(solution)/shard_map/all_to_all | solution.py:151
  128.7 13.8 %copy-start.9 = (bf16[512,128]{1,0:T(8,128)(2,1)S(1)}, bf16[512,128]{1,0:T(8,128)(2,1)}, u32[]{:S(2)}) copy-start(bf16[512,128]{1,0:T(8,128)(2,1)} %copy-done.8) | copy-start | bytes 393220
  139.0 20.0 %all-to-all-start.4 = ((bf16[8,128,128]{2,1,0:T(8,128)(2,1)}), bf16[8,128,128]{2,1,0:T(8,128)(2,1)S(1)}, u32[]{:S(2)}, u32[]{:S(2)}) async-start(bf16[8,128,128]{2,1,0:T(8,128)(2,1)} %bitcast.23), calls=%async_computation.4 | async-start | bytes 524288 | tf_op jit(solution)/shard_map/all_to_all | solution.py:150
  159.0 31.6 %all-to-all-start.3 = ((bf16[8,128,128]{1,2,0:T(8,128)(2,1)}), bf16[8,128,128]{1,2,0:T(8,128)(2,1)S(1)}, u32[]{:S(2)}, u32[]{:S(2)}) async-start(bf16[8,128,128]{1,2,0:T(8,128)(2,1)} %copy.27), calls=%async_computation.3 | async-start | bytes 524288 | tf_op jit(solution)/shard_map/all_to_all | solution.py:113
  166.4 27.1 %copy-start.11 = (bf16[1,256,1024]{2,1,0:T(8,128)(2,1)}, bf16[1,256,1024]{2,1,0:T(8,128)(2,1)S(1)}, u32[]{:S(2)}) copy-start(bf16[1,256,1024]{2,1,0:T(8,128)(2,1)S(1)} %dynamic_update_slice.15) | copy-start | bytes 1572868
  168.3 25.2 %copy-start.12 = (bf16[1,256,1024]{2,1,0:T(8,128)(2,1)}, bf16[1,256,1024]{2,1,0:T(8,128)(2,1)S(1)}, u32[]{:S(2)}) copy-start(bf16[1,256,1024]{2,1,0:T(8,128)(2,1)S(1)} %dynamic_update_slice.14) | copy-start | bytes 1572868
  170.1 20.4 %copy-start.13 = (bf16[1,256,1024]{2,1,0:T(8,128)(2,1)}, bf16[1,256,1024]{2,1,0:T(8,128)(2,1)S(1)}, u32[]{:S(2)}) copy-start(bf16[1,256,1024]{2,1,0:T(8,128)(2,1)S(1)} %dynamic_update_slice.13) | copy-start | bytes 1572868
  196.5 20.9 %copy-start.10 = (bf16[1,256,2048]{2,1,0:T(8,128)(2,1)}, bf16[1,256,2048]{2,1,0:T(8,128)(2,1)S(1)}, u32[]{:S(2)}) copy-start(bf16[1,256,2048]{2,1,0:T(8,128)(2,1)S(1)} %dynamic_update_slice.12) | copy-start | bytes 3145732
  (5 other events, 8.4 us)
Sparse Core Ops, SparseCore 0:
  12.1 86.4 all-gather.5
  100.7 89.7 all-gather.3
  193.6 23.7 reduce-scatter.1
where the time goes:
time: 225 us; the launch traced here: 224 us
  waiting for transfers between devices  121 us (54%)
  starting transfers between devices  29.8 us (13%)
  matrix products  20.6 us (9%)
  between operations  15.6 us (7%)
  local copies, waits for them, and re-layouts  14.9 us (7%)
  other arithmetic  11.8 us (5%)
  blocking collectives  10.2 us (5%)
    reduce_scatter x1, waiting for transfers between devices, shards(): lax.psum_scatter(weight_term, 'dp', scatter_dimension=1, tiled=True)  20.9 us
    all_gather x1, waiting for transfers between devices, shards(): full_proj = lax.all_gather(head_rows, 'ctx', axis=0, tiled=True)  20.4 us
    all_to_all x1, waiting for transfers between devices, shards(): lax.all_to_all(v_slot, 'ctx', split_axis=1, concat_axis=0, tiled=True)  15.9 us
    all_to_all x1, waiting for transfers between devices, shards(): lax.all_to_all(q_heads_grad, 'ctx', split_axis=0, concat_axis=1, tiled=True)  15.6 us
    all_to_all x1, waiting for transfers between devices, shards(): lax.all_to_all(k_slot, 'ctx', split_axis=1, concat_axis=0, tiled=True)  15.6 us
    all_to_all x1, waiting for transfers between devices, shards(): lax.all_to_all(q_slot, 'ctx', split_axis=1, concat_axis=0, tiled=True)  12.3 us
    all_gather x1, blocking collectives, shards(): head_rows = lax.all_gather(proj, 'dp', axis=1, tiled=True)  10.2 us
    dot_general x5, matrix products, cross_dot(): lax.dot_general(left_op, right_op, (((1,), (1,)), ((), ())), preferred_el...  8.96 us
  transfers between devices with their start and end apart: 10, of which 9 were waited for; matrix products, arithmetic and copies ran while one was open for 19% of the time, Pallas kernels for 0%

commit v1 on v0

v1 whole, which is shorter than its diff:
```python
import functools
import math

import jax
import jax.numpy as jnp
from jax import lax
from jax.experimental import pallas as pl
from jax.experimental.pallas import tpu as pltpu
from jax.sharding import PartitionSpec as P

BLOCK = 128
FAR = 1 << 30


def dot_nt(a, b):
    return lax.dot_general(a, b, (((1,), (1,)), ((), ())), preferred_element_type=jnp.float32)


def dot_nn(a, b):
    return lax.dot_general(a, b, (((1,), (0,)), ((), ())), preferred_element_type=jnp.float32)


def transposed(a):
    return a.astype(jnp.float32).T.astype(a.dtype)


def kernel(
    n, dn, scale,
    qkv, g, proj, kpos, qrow,
    dq_r, dkv_r, w_out, mix_r,
    qkv_r, g_r, proj_r, agp_s, agp_r, ag_s, ag_r, attn_s, attn_r, attn_d, attn_t,
    p_s, k_t, v_t, dq_s, dkv_s, dk_acc, dv_acc, w_s, w_r, mix_s,
    qkv_ss, qkv_rs, g_ss, g_rs, proj_ss, proj_rs, fwd_ss, agp_ss, agp_rs, ag_ss, ag_rs,
    attn_ss, attn_rs, ad_ss, ad_rs, dq_ss, dq_rs, dkv_ss, dkv_rs, w_ss, w_rs, mix_ss, mix_rs,
    loc,
):
    me = lax.axis_index("ctx")
    md = lax.axis_index("dp")
    bf16 = jnp.bfloat16
    block, dh = qkv.shape[2], qkv.shape[3]
    dc = proj.shape[1]
    slots = n * block
    width = 2 * block
    steps = n // 2

    def ctx_copy(src, dst, ss, rs, peer):
        return pltpu.make_async_remote_copy(
            src_ref=src, dst_ref=dst, send_sem=ss, recv_sem=rs,
            device_id={"ctx": peer}, device_id_type=pl.DeviceIdType.MESH)

    def dp_copy(src, dst, ss, rs, peer):
        return pltpu.make_async_remote_copy(
            src_ref=src, dst_ref=dst, send_sem=ss, recv_sem=rs,
            device_id={"dp": peer}, device_id_type=pl.DeviceIdType.MESH)

    ctx_peers = [lax.rem(me + s, n) for s in range(1, n)]
    dp_peers = [lax.rem(md + s, dn) for s in range(1, dn)]

    barrier = pltpu.get_barrier_semaphore()
    for peer in ctx_peers:
        pl.semaphore_signal(barrier, inc=1, device_id={"ctx": peer}, device_id_type=pl.DeviceIdType.MESH)
    for peer in dp_peers:
        pl.semaphore_signal(barrier, inc=1, device_id={"dp": peer}, device_id_type=pl.DeviceIdType.MESH)

    own = [
        pltpu.make_async_copy(qkv.at[me], qkv_r.at[me], loc.at[0]),
        pltpu.make_async_copy(g.at[md], g_r.at[md], loc.at[1]),
        pltpu.make_async_copy(proj, proj_r.at[me], loc.at[2]),
    ]
    for copy in own:
        copy.start()
    pl.semaphore_wait(barrier, n - 1 + dn - 1)

    pair = me + 1 - 2 * lax.rem(me, 2)
    far = [lax.rem(me + 2 * s, n) for s in range(1, n // 2)]
    sends = []

    def go(copy):
        copy.start()
        sends.append(copy)

    for peer in far + [pair]:
        go(ctx_copy(proj, proj_r.at[me], proj_ss.at[peer], proj_rs.at[me], peer))
    for peer in dp_peers:
        go(dp_copy(g.at[peer], g_r.at[md], g_ss.at[peer], g_rs.at[md], peer))
    for peer in ctx_peers:
        go(ctx_copy(qkv.at[peer], qkv_r.at[me], qkv_ss.at[peer], qkv_rs.at[me], peer))
    for copy in own:
        copy.wait()

    def ctx_arrived(buf, ss, rs, peer):
        ctx_copy(buf.at[peer], buf.at[peer], ss.at[peer], rs.at[peer], peer).wait_recv()

    def dp_arrived(buf, ss, rs, peer):
        dp_copy(buf.at[peer], buf.at[peer], ss.at[peer], rs.at[peer], peer).wait_recv()

    for peer in far:
        ctx_arrived(proj_r, proj_ss, proj_rs, peer)
        go(ctx_copy(proj_r.at[peer], proj_r.at[peer], fwd_ss.at[peer], proj_rs.at[peer], pair))
    for peer in [pair] + [lax.rem(pair + 2 * s, n) for s in range(1, n // 2)]:
        ctx_arrived(proj_r, proj_ss, proj_rs, peer)
    for peer in dp_peers:
        dp_arrived(g_r, g_ss, g_rs, peer)

    def part_step(j, carry):
        heads = proj_r[pl.ds(2 * j, 2)].reshape(2 * dh, dc)
        out = dot_nt(g_r[...].reshape(dn * block, dc), heads).astype(bf16)
        agp_s[:, pl.ds(2 * j, 1)] = out[:, :dh].reshape(dn, 1, block, dh)
        agp_s[:, pl.ds(2 * j + 1, 1)] = out[:, dh:].reshape(dn, 1, block, dh)
        return carry

    lax.fori_loop(0, steps, part_step, 0)
    for peer in dp_peers:
        go(dp_copy(agp_s.at[peer], agp_r.at[md], agp_ss.at[peer], agp_rs.at[md], peer))

    for peer in ctx_peers:
        ctx_arrived(qkv_r, qkv_ss, qkv_rs, peer)
    k_t[...] = transposed(qkv_r[:, 1].reshape(slots, dh))
    v_t[...] = transposed(qkv_r[:, 2].reshape(slots, dh))

    for peer in dp_peers:
        dp_arrived(agp_r, agp_ss, agp_rs, peer)

    def sum_step(h, carry):
        total = agp_s[md, h].astype(jnp.float32)
        for peer in dp_peers:
            total = total + agp_r[peer, h].astype(jnp.float32)
        ag_s[h] = total.astype(bf16)
        return carry

    lax.fori_loop(0, n, sum_step, 0)
    for peer in ctx_peers:
        go(ctx_copy(ag_s.at[peer], ag_r.at[me], ag_ss.at[peer], ag_rs.at[me], peer))
    ag_r[me] = ag_s[me]

    def send_pair(i, src, dst, ss, rs, own_sem):
        for half in range(2):
            peer = 2 * i + half

            @pl.when(peer != me)
            def _():
                ctx_copy(src.at[peer], dst.at[me], ss.at[peer], rs.at[me], peer).start()

            @pl.when(peer == me)
            def _():
                pltpu.make_async_copy(src.at[peer], dst.at[peer], own_sem).start()

    def forward(i, carry):
        q = qkv_r[pl.ds(2 * i, 2), 0].reshape(width, dh)
        k = qkv_r[:, 1].reshape(slots, dh)
        scores = dot_nt(k, q) * scale
        key_pos = kpos[...]
        key_pos = jnp.concatenate([key_pos, key_pos], axis=1)
        same = lax.broadcasted_iota(jnp.int32, (slots, width), 0) == (
            lax.broadcasted_iota(jnp.int32, (slots, width), 1) + i * width)
        scores = jnp.where((key_pos <= qrow[i]) | same, scores, -1e30)
        e = jnp.exp(scores - jnp.max(scores, axis=0, keepdims=True))
        p = (e * (1.0 / jnp.sum(e, axis=0, keepdims=True))).astype(bf16)
        p_s[i] = p
        a_t = dot_nn(v_t[...], p)
        attn_t[i] = a_t.astype(bf16)
        attn_s[pl.ds(2 * i, 2)] = a_t.T.astype(bf16).reshape(2, block, dh)
        send_pair(i, attn_s, attn_r, attn_ss, attn_rs, loc.at[3])
        return carry

    lax.fori_loop(0, steps, forward, 0)

    for peer in ctx_peers:
        ctx_arrived(ag_r, ag_ss, ag_rs, peer)
    dk_acc[...] = jnp.zeros_like(dk_acc)
    dv_acc[...] = jnp.zeros_like(dv_acc)

    def backward(i, carry):
        q = qkv_r[pl.ds(2 * i, 2), 0].reshape(width, dh)
        v = qkv_r[:, 2].reshape(slots, dh)
        da = ag_r[pl.ds(2 * i, 2)].reshape(width, dh)
        delta = jnp.sum(da.astype(jnp.float32).T * attn_t[i].astype(jnp.float32), axis=0, keepdims=True)
        p = p_s[i]
        ds = (p.astype(jnp.float32) * (dot_nt(v, da) - delta)).astype(bf16)
        dq_t = dot_nn(k_t[...], ds) * scale
        dq_s[pl.ds(2 * i, 2)] = dq_t.T.astype(bf16).reshape(2, block, dh)
        send_pair(i, dq_s, dq_r, dq_ss, dq_rs, loc.at[4])
        dk_acc[...] += dot_nn(ds, q)
        dv_acc[...] += dot_nn(p, da)
        return carry

    early = steps // 2
    lax.fori_loop(0, early, backward, 0)
    for peer in ctx_peers:
        ctx_arrived(attn_r, attn_ss, attn_rs, peer)
    pltpu.make_async_copy(attn_s.at[me], attn_r.at[me], loc.at[3]).wait()
    for peer in dp_peers:
        go(dp_copy(attn_r, attn_d.at[md], ad_ss.at[peer], ad_rs.at[md], peer))
    own_attn = pltpu.make_async_copy(attn_r, attn_d.at[md], loc.at[5])
    own_attn.start()
    lax.fori_loop(early, steps, backward, 0)

    dkv_s[:, 0] = (dk_acc[...] * scale).astype(bf16).reshape(n, block, dh)
    dkv_s[:, 1] = dv_acc[...].astype(bf16).reshape(n, block, dh)
    for peer in ctx_peers:
        go(ctx_copy(dkv_s.at[peer], dkv_r.at[me], dkv_ss.at[peer], dkv_rs.at[me], peer))
    dkv_r[me] = dkv_s[me]

    own_attn.wait()
    for peer in dp_peers:
        dp_arrived(attn_d, ad_ss, ad_rs, peer)

    def weight_step(s, carry):
        h = lax.rem(me + s, n)
        heads = attn_d[:, h].reshape(dn * block, dh)
        w_s[h] = dot_nn(transposed(heads), g_r[...].reshape(dn * block, dc)).astype(bf16)

        @pl.when(s != 0)
        def _():
            ctx_copy(w_s.at[h], w_r.at[me], w_ss.at[h], w_rs.at[me], h).start()

        return carry

    lax.fori_loop(0, n, lambda s, carry: weight_step(n - 1 - s, carry), 0)

    def mix_step(j, carry):
        rows = jnp.concatenate(
            [attn_d[pl.ds(2 * j, 2), h].reshape(width, dh) for h in range(n)], axis=1)
        out = dot_nn(rows, proj_r[...].reshape(n * dh, dc))
        mix_s[pl.ds(2 * j, 2)] = out.astype(bf16).reshape(2, block, dc)
        return carry

    lax.fori_loop(0, dn // 2, mix_step, 0)
    for peer in dp_peers:
        go(dp_copy(mix_s.at[peer], mix_r.at[md], mix_ss.at[peer], mix_rs.at[md], peer))
    mix_r[md] = mix_s[md]

    pltpu.make_async_copy(dq_s.at[me], dq_r.at[me], loc.at[4]).wait()
    for peer in ctx_peers:
        ctx_arrived(dq_r, dq_ss, dq_rs, peer)
    for peer in ctx_peers:
        ctx_arrived(dkv_r, dkv_ss, dkv_rs, peer)
    for peer in ctx_peers:
        ctx_arrived(w_r, w_ss, w_rs, peer)
    total = w_s[me].astype(jnp.float32)
    for peer in ctx_peers:
        total = total + w_r[peer].astype(jnp.float32)
    w_out[...] = total
    for peer in dp_peers:
        dp_arrived(mix_r, mix_ss, mix_rs, peer)

    for copy in sends:
        copy.wait_send()
    for peer in ctx_peers:
        ctx_copy(attn_s.at[peer], attn_r.at[me], attn_ss.at[peer], attn_rs.at[me], peer).wait_send()
        ctx_copy(dq_s.at[peer], dq_r.at[me], dq_ss.at[peer], dq_rs.at[me], peer).wait_send()
        ctx_copy(w_s.at[peer], w_r.at[me], w_ss.at[peer], w_rs.at[me], peer).wait_send()


def shards(queries, keys, values, out_grad, chosen, proj):
    n = lax.axis_size("ctx")
    dn = lax.axis_size("dp")
    me = lax.axis_index("ctx")
    tokens = queries.shape[1]
    half_rows = tokens // 2
    picked = chosen[0]
    own_pick = lax.dynamic_index_in_dim(picked, me, 0, keepdims=False)
    own_live = own_pick >= 0
    first_pos = jnp.where(own_live, own_pick, 0) * BLOCK
    local_row = jnp.where(
        first_pos // half_rows == me,
        first_pos % half_rows,
        half_rows + first_pos % half_rows,
    )
    row_start = jnp.where(own_live, local_row, 0)

    def take_rows(source):
        slot_block = lax.dynamic_slice_in_dim(source[0], row_start, BLOCK, 0)
        return jnp.where(own_live, slot_block, jnp.zeros((), source.dtype))

    dh = queries.shape[2] // n
    dc = proj.shape[1]
    slots = n * BLOCK
    width = 2 * BLOCK
    steps = n // 2

    def by_head(rows):
        return rows.reshape(BLOCK, n, dh).transpose(1, 0, 2)

    qkv = jnp.stack([by_head(take_rows(x)) for x in (queries, keys, values)], axis=1)
    g = take_rows(out_grad).reshape(BLOCK, dn, dc).transpose(1, 0, 2)

    offsets = jnp.arange(BLOCK, dtype=jnp.int32)
    live = picked >= 0
    pos = (picked[:, None] * BLOCK + offsets[None, :])
    key_pos = jnp.where(live[:, None], pos, FAR).reshape(slots)
    query_pos = jnp.where(live[:, None], pos, -1).reshape(steps, 1, width)
    key_pos = jnp.broadcast_to(key_pos[:, None], (slots, BLOCK))

    bf16, f32 = jnp.bfloat16, jnp.float32
    sem = pltpu.SemaphoreType.DMA
    vm = pltpu.VMEM
    blocks = (n, BLOCK, dh)
    scratch = [
        vm((n, 3, BLOCK, dh), bf16), vm((dn, BLOCK, dc), bf16), vm((n, dh, dc), bf16),
        vm((dn,) + blocks, bf16), vm((dn,) + blocks, bf16), vm(blocks, bf16), vm(blocks, bf16),
        vm(blocks, bf16), vm(blocks, bf16), vm((dn,) + blocks, bf16), vm((steps, dh, width), bf16),
        vm((steps, slots, width), bf16), vm((dh, slots), bf16), vm((dh, slots), bf16),
        vm(blocks, bf16), vm((n, 2, BLOCK, dh), bf16), vm((slots, dh), f32), vm((slots, dh), f32),
        vm((n, dh, dc), bf16), vm((n, dh, dc), bf16), vm((dn, BLOCK, dc), bf16),
    ]
    c, d = sem((n,)), sem((dn,))
    sems = [c, c, d, d, c, c, c, d, d, c, c, c, c, d, d, c, c, c, c, c, c, d, d, sem((6,))]
    dq, dkv, proj_grad, mixed = pl.pallas_call(
        functools.partial(kernel, n, dn, 1.0 / math.sqrt(dh)),
        out_shape=(
            jax.ShapeDtypeStruct(blocks, bf16),
            jax.ShapeDtypeStruct((n, 2, BLOCK, dh), bf16),
            jax.ShapeDtypeStruct((dh, dc), f32),
            jax.ShapeDtypeStruct((dn, BLOCK, dc), bf16),
        ),
        in_specs=[pl.BlockSpec(memory_space=pltpu.VMEM)] * 5,
        out_specs=[pl.BlockSpec(memory_space=pltpu.VMEM)] * 4,
        scratch_shapes=scratch + sems,
        compiler_params=pltpu.CompilerParams(
            collective_id=0, has_side_effects=True, vmem_limit_bytes=60 * 1024 * 1024),
    )(qkv, g, proj, key_pos, query_pos)

    count = tokens // BLOCK
    here = (jnp.arange(count, dtype=jnp.int32) == row_start // BLOCK) & own_live

    def place(rows):
        out = jnp.where(here[:, None, None], rows[None], jnp.zeros((), rows.dtype))
        return out.reshape(1, tokens, rows.shape[1])

    def rows_of(parts):
        return parts.transpose(1, 0, 2).reshape(BLOCK, parts.shape[0] * parts.shape[2])

    return (
        place(rows_of(mixed)),
        place(rows_of(dq)),
        place(rows_of(dkv[:, 0])),
        place(rows_of(dkv[:, 1])),
        proj_grad,
    )


def solution(mesh):
    rows = P("dp", "ctx", None)
    return jax.shard_map(
        shards,
        mesh=mesh,
        in_specs=(rows, rows, rows, rows, P("dp", None), P("ctx", "dp")),
        out_specs=(rows, rows, rows, rows, P("ctx", "dp")),
        check_vma=False,
    )
```

time: 225 us -> 119 us (0.53)
  waiting for transfers between devices: 121 us -> 0 us
  Pallas kernels: 0 us -> 100 us
  starting transfers between devices: 29.8 us -> 0 us
  matrix products: 20.6 us -> 0 us
  between operations: 15.6 us -> 2.27 us
  blocking collectives: 10.2 us -> 0 us
  other arithmetic: 11.8 us -> 4.23 us
  local copies, waits for them, and re-layouts: 14.9 us -> 11.6 us
    pallas_call x0 -> x1, Pallas kernels: none -> 100 us  [shards(): pl.pallas_call(functools.partial(kernel, n, dn, 1.0 / math.sqrt(dh)), out...]
    all_to_all x7 -> x0, waiting for transfers between devices: 75.6 us -> none  [the longest x1 15.9 us: shards(): lax.all_to_all(v_slot, 'ctx', split_axis=1, concat_axis=0, tiled=True)]
    all_to_all x7 -> x0, starting transfers between devices: 29.7 us -> none  [the longest x1 5.83 us: shards(): lax.all_to_all(k_slot, 'ctx', split_axis=1, concat_axis=0, tiled=True)]
    all_gather x2 -> x0, waiting for transfers between devices: 24.4 us -> none  [the longest x1 20.4 us: shards(): full_proj = lax.all_gather(head_rows, 'ctx', axis=0, tiled=True)]
    reduce_scatter x1 -> x0, waiting for transfers between devices: 20.9 us -> none  [shards(): lax.psum_scatter(weight_term, 'dp', scatter_dimension=1, tiled=True)]
    dot_general x15 -> x0, matrix products: 20.6 us -> none  [the longest x5 8.96 us: cross_dot(): lax.dot_general(left_op, right_op, (((1,), (1,)), ((), ())), preferred_el...]
    all_gather x1 -> x0, blocking collectives: 10.2 us -> none  [shards(): head_rows = lax.all_gather(proj, 'dp', axis=1, tiled=True)]
    dynamic_update_slice x4 -> x0, local copies, waits for them, and re-layouts: 8.22 us -> none  [place_rows(): lax.dynamic_update_slice_in_dim(jnp.zeros(template.shape, jnp.bfloat16),...]
  transfers between devices with their start and end apart: 10 -> 0, of which waited for: 9 -> 0; matrix products, arithmetic and copies ran while one was open for 19% -> 0% of each run, Pallas kernels for 0% -> 0%
where the time goes in v1:
time: 119 us
  Pallas kernels  100 us (84%)
  local copies, waits for them, and re-layouts  11.6 us (10%)
  other arithmetic  4.23 us (4%)
  between operations  2.27 us (2%)
    pallas_call x1, Pallas kernels, shards(): pl.pallas_call(functools.partial(kernel, n, dn, 1.0 / math.sqrt(dh)), out...  100 us
    unnamed x19, local copies, waits for them, and re-layouts  3.78 us
    select_n x2, other arithmetic, place(): out = jnp.where(here[:, None, None], rows[None], jnp.zeros((), rows.dtype))  2.43 us

profile of v1, /device:TPU:0, one launch (start us, length us, event | category | flops | bytes accessed | tf_op | source)
XLA Modules:
  0.0 118.6 jit_solution(13365038940919693574)
XLA Ops:
  0.7 0.7 copy-done.6
  1.4 0.6 constant_dynamic-slice_fusion.4
  3.3 1.1 constant_dynamic-slice_fusion.2
  4.4 0.2 copy.30
  4.9 0.2 copy.16
  5.1 0.2 copy.14
  5.3 0.7 copy-done.5
  6.2 0.2 copy.12
  6.4 1.0 pad_maximum_fusion.qkv
  7.5 0.3 copy.32
  7.9 1.0 copy.18
  9.0 1.0 broadcast_in_dim.129.kpos
  10.4 0.6 copy_select_fusion.qrow
  11.0 100.5 %shard_map.101 = (bf16[8,128,128]{2,1,0:T(8,128)(2,1)}, bf16[8,2,128,128]{3,2,1,0:T(8,128)(2,1)}, f32[128,512]{1,0:T(8,128)}, bf16[4,128,512]{2,1,0:T(8,128)(2,1)}) custom-call(bf16[8,3,128,128]{3,2,1,0:T(8,128)(2,1)} %pad_maximum_fusion.qkv, bf16[4,128,512]{2,1,0:T(8,128)(2,1)} %bitcast.58, bf16[128,512]{1,0:T(8,128)(2,1)} %proj.1, ...), custom_call_target="tpu_custom_call" | custom-call | tf_op jit(solution)/shard_map/pallas_call | solution.py:309
  111.5 1.1 slice_bitcast_fusion
  112.6 0.2 copy.25
  113.0 0.2 copy.27
  113.4 0.9 copy-done.3
  114.3 0.2 copy.23
  114.8 1.3 %bitcast_select_fusion.1 = (bf16[1,256,1024]{2,1,0:T(8,128)(2,1)}, bf16[1,256,1024]{2,1,0:T(8,128)(2,1)}, bf16[1,256,1024]{2,1,0:T(8,128)(2,1)}) fusion(pred[256]{0:T(512)(128)(4,1)S(1)} %broadcast_bitcast_fusion.1, bf16[1,256,1024]{2,1,0:T(8,128)(2,1)S(1)} %bitcast.56, bf16[1,256,1024]{2,1,0:T(8,128)(2,1)S(1)} %bitcast.55, bf16[1,256,1024]{2,1,0:T(8,128)(2,1)S(1)} %bitcast.57), kind=kLoop, calls=%fused_computation.2 | loop fusion | flops 786432 | bytes 3145984 | tf_op jit(solution)/shard_map/jit(_where)/select_n | solution.py:328
  116.1 0.3 copy.21
  116.4 0.2 copy.22
  116.7 1.1 bitcast_select_fusion
  117.9 0.7 copy.35
  (37 shorter events, 2.1 us)
Async XLA Ops:
  0.6 6.8 %copy-start = (bf16[1,256,2048]{2,1,0:T(8,128)(2,1)S(1)}, bf16[1,256,2048]{2,1,0:T(8,128)(2,1)}, u32[]{:S(2)}) copy-start(bf16[1,256,2048]{2,1,0:T(8,128)(2,1)} %param.9) | copy-start | bytes 3145732
  0.7 0.7 copy-start.6
  3.3 1.3 %copy-start.4 = (bf16[1,256,1024]{2,1,0:T(8,128)(2,1)S(1)}, bf16[1,256,1024]{2,1,0:T(8,128)(2,1)}, u32[]{:S(2)}) copy-start(bf16[1,256,1024]{2,1,0:T(8,128)(2,1)} %param.8) | copy-start | bytes 1572868
  4.9 1.0 copy-start.5
  113.3 1.0 copy-start.3
  114.8 1.3 %copy-start.1 = (bf16[4,128,512]{2,1,0:T(8,128)(2,1)S(1)}, bf16[4,128,512]{2,1,0:T(8,128)(2,1)}, u32[]{:S(2)}) copy-start(bf16[4,128,512]{2,1,0:T(8,128)(2,1)} %get-tuple-element.9) | copy-start | bytes 1572868
  116.7 1.1 copy-start.2

commit v2 on v1

--- a/solution.py
+++ b/solution.py
@@ -24,14 +24,39 @@
     return a.astype(jnp.float32).T.astype(a.dtype)
 
 
+def block_marks(picked, me, count):
+    entry = picked[0, me]
+    spans = count // 2
+    index = jnp.maximum(entry, 0)
+    local = jnp.where(index // spans == me, index % spans, spans + index % spans)
+    local = jnp.where(entry >= 0, local, -1)
+    return [jnp.where(local == j, 1.0, 0.0) for j in range(count)]
+
+
+def place_kernel(n, dn, count, picked, mix, dq, dkv, w, out, q_out, k_out, v_out, w_out):
+    marks = block_marks(picked, lax.axis_index("ctx"), count)
+    block, dh, dc = dq.shape[1], dq.shape[2], mix.shape[2]
+    for j, mark in enumerate(marks):
+        rows = slice(j * block, (j + 1) * block)
+        for h in range(n):
+            cols = slice(h * dh, (h + 1) * dh)
+            q_out[rows, cols] = (dq[h].astype(jnp.float32) * mark).astype(q_out.dtype)
+            k_out[rows, cols] = (dkv[h, 0].astype(jnp.float32) * mark).astype(k_out.dtype)
+            v_out[rows, cols] = (dkv[h, 1].astype(jnp.float32) * mark).astype(v_out.dtype)
+        for d in range(dn):
+            cols = slice(d * dc, (d + 1) * dc)
+            out[rows, cols] = (mix[d].astype(jnp.float32) * mark).astype(out.dtype)
+    w_out[...] = w[...]
+
+
 def kernel(
     n, dn, scale,
-    qkv, g, proj, kpos, qrow,
+    picked, q_in, k_in, v_in, g_in, proj,
     dq_r, dkv_r, w_out, mix_r,
-    qkv_r, g_r, proj_r, agp_s, agp_r, ag_s, ag_r, attn_s, attn_r, attn_d, attn_t,
-    p_s, k_t, v_t, dq_s, dkv_s, dk_acc, dv_acc, w_s, w_r, mix_s,
+    qkv, g, kpos, qkv_r, g_r, proj_r, agp_s, agp_r, ag_s, ag_r, attn_s, attn_r, attn_d, attn_t,
+    p_s, k_t, v_t, dq_s, dkv_s, dk_acc, dv_acc, w_s, w_y, w_r, mix_s,
     qkv_ss, qkv_rs, g_ss, g_rs, proj_ss, proj_rs, fwd_ss, agp_ss, agp_rs, ag_ss, ag_rs,
-    attn_ss, attn_rs, ad_ss, ad_rs, dq_ss, dq_rs, dkv_ss, dkv_rs, w_ss, w_rs, mix_ss, mix_rs,
+    attn_ss, attn_rs, ad_ss, ad_rs, ad_fs, dq_ss, dq_rs, dkv_ss, dkv_rs, w_ss, wy_rs, w_rs, mix_ss, mix_rs,
     loc,
 ):
     me = lax.axis_index("ctx")
@@ -62,17 +87,20 @@
     for peer in dp_peers:
         pl.semaphore_signal(barrier, inc=1, device_id={"dp": peer}, device_id_type=pl.DeviceIdType.MESH)
 
-    own = [
-        pltpu.make_async_copy(qkv.at[me], qkv_r.at[me], loc.at[0]),
-        pltpu.make_async_copy(g.at[md], g_r.at[md], loc.at[1]),
-        pltpu.make_async_copy(proj, proj_r.at[me], loc.at[2]),
-    ]
-    for copy in own:
-        copy.start()
-    pl.semaphore_wait(barrier, n - 1 + dn - 1)
+    own_proj = pltpu.make_async_copy(proj, proj_r.at[me], loc.at[2])
+    own_proj.start()
+    marks = block_marks(picked, me, q_in.shape[0] // block)
+
+    def chosen_rows(ref, low, high):
+        total = None
+        for j, mark in enumerate(marks):
+            term = ref[j * block:(j + 1) * block, low:high].astype(jnp.float32) * mark
+            total = term if total is None else total + term
+        return total.astype(bf16)
 
     pair = me + 1 - 2 * lax.rem(me, 2)
     far = [lax.rem(me + 2 * s, n) for s in range(1, n // 2)]
+    pl.semaphore_wait(barrier, n - 1 + dn - 1)
     sends = []
 
     def go(copy):
@@ -81,12 +109,20 @@
 
     for peer in far + [pair]:
         go(ctx_copy(proj, proj_r.at[me], proj_ss.at[peer], proj_rs.at[me], peer))
+    for j in range(dn):
+        g[j] = chosen_rows(g_in, j * dc, (j + 1) * dc)
     for peer in dp_peers:
         go(dp_copy(g.at[peer], g_r.at[md], g_ss.at[peer], g_rs.at[md], peer))
-    for peer in ctx_peers:
-        go(ctx_copy(qkv.at[peer], qkv_r.at[me], qkv_ss.at[peer], qkv_rs.at[me], peer))
-    for copy in own:
-        copy.wait()
+    g_r[md] = g[md]
+    for t, ref in enumerate((q_in, k_in, v_in)):
+        for h in range(n):
+            qkv[h, t] = chosen_rows(ref, h * dh, (h + 1) * dh)
+    qkv_r[me] = qkv[me]
+    down = lax.broadcasted_iota(jnp.int32, (block, block), 0)
+    for j in range(n):
+        entry = picked[0, j]
+        kpos[j * block:(j + 1) * block] = down + jnp.where(entry >= 0, entry * block, FAR)
+    own_proj.wait()
 
     def ctx_arrived(buf, ss, rs, peer):
         ctx_copy(buf.at[peer], buf.at[peer], ss.at[peer], rs.at[peer], peer).wait_recv()
@@ -97,6 +133,8 @@
     for peer in far:
         ctx_arrived(proj_r, proj_ss, proj_rs, peer)
         go(ctx_copy(proj_r.at[peer], proj_r.at[peer], fwd_ss.at[peer], proj_rs.at[peer], pair))
+    for peer in ctx_peers:
+        go(ctx_copy(qkv.at[peer], qkv_r.at[me], qkv_ss.at[peer], qkv_rs.at[me], peer))
     for peer in [pair] + [lax.rem(pair + 2 * s, n) for s in range(1, n // 2)]:
         ctx_arrived(proj_r, proj_ss, proj_rs, peer)
     for peer in dp_peers:
@@ -153,7 +191,12 @@
         key_pos = jnp.concatenate([key_pos, key_pos], axis=1)
         same = lax.broadcasted_iota(jnp.int32, (slots, width), 0) == (
             lax.broadcasted_iota(jnp.int32, (slots, width), 1) + i * width)
-        scores = jnp.where((key_pos <= qrow[i]) | same, scores, -1e30)
+        lane = lax.broadcasted_iota(jnp.int32, (1, width), 1)
+        first, second = picked[0, 2 * i], picked[0, 2 * i + 1]
+        first = jnp.where(first >= 0, first * block, -FAR)
+        second = jnp.where(second >= 0, (second - 1) * block, -FAR)
+        query_pos = lane + jnp.where(lane < block, first, second)
+        scores = jnp.where((key_pos <= query_pos) | same, scores, -1e30)
         e = jnp.exp(scores - jnp.max(scores, axis=0, keepdims=True))
         p = (e * (1.0 / jnp.sum(e, axis=0, keepdims=True))).astype(bf16)
         p_s[i] = p
@@ -189,7 +232,9 @@
     for peer in ctx_peers:
         ctx_arrived(attn_r, attn_ss, attn_rs, peer)
     pltpu.make_async_copy(attn_s.at[me], attn_r.at[me], loc.at[3]).wait()
-    for peer in dp_peers:
+    twin = md + 1 - 2 * lax.rem(md, 2)
+    dp_far = [lax.rem(md + 2 * s, dn) for s in range(1, dn // 2)]
+    for peer in dp_far + [twin]:
         go(dp_copy(attn_r, attn_d.at[md], ad_ss.at[peer], ad_rs.at[md], peer))
     own_attn = pltpu.make_async_copy(attn_r, attn_d.at[md], loc.at[5])
     own_attn.start()
@@ -202,21 +247,23 @@
     dkv_r[me] = dkv_s[me]
 
     own_attn.wait()
-    for peer in dp_peers:
+    for peer in dp_far:
         dp_arrived(attn_d, ad_ss, ad_rs, peer)
-
-    def weight_step(s, carry):
-        h = lax.rem(me + s, n)
+        go(dp_copy(attn_d.at[peer], attn_d.at[peer], ad_fs.at[peer], ad_rs.at[peer], twin))
+    for peer in [twin] + [lax.rem(twin + 2 * s, dn) for s in range(1, dn // 2)]:
+        dp_arrived(attn_d, ad_ss, ad_rs, peer)
+
+    def weight(h):
         heads = attn_d[:, h].reshape(dn * block, dh)
-        w_s[h] = dot_nn(transposed(heads), g_r[...].reshape(dn * block, dc)).astype(bf16)
-
-        @pl.when(s != 0)
-        def _():
-            ctx_copy(w_s.at[h], w_r.at[me], w_ss.at[h], w_rs.at[me], h).start()
-
-        return carry
-
-    lax.fori_loop(0, n, lambda s, carry: weight_step(n - 1 - s, carry), 0)
+        return dot_nn(transposed(heads), g_r[...].reshape(dn * block, dc))
+
+    side = lax.rem(me, 2)
+    row = me // 2
+    orders = [lax.rem(row + s, n // 2) for s in range(1, n // 2)] + [row]
+    for a in orders:
+        h = 2 * a + 1 - side
+        w_s[h] = weight(h).astype(bf16)
+        go(ctx_copy(w_s.at[h], w_y.at[a], w_ss.at[h], wy_rs.at[a], pair))
 
     def mix_step(j, carry):
         rows = jnp.concatenate(
@@ -230,17 +277,25 @@
         go(dp_copy(mix_s.at[peer], mix_r.at[md], mix_ss.at[peer], mix_rs.at[md], peer))
     mix_r[md] = mix_s[md]
 
+    for a in orders:
+        h = 2 * a + side
+        total = weight(h)
+        ctx_copy(w_y.at[a], w_y.at[a], w_ss.at[h], wy_rs.at[a], pair).wait_recv()
+        total = total + w_y[a].astype(jnp.float32)
+        if a is row:
+            w_out[...] = total
+        else:
+            w_s[h] = total.astype(bf16)
+            go(ctx_copy(w_s.at[h], w_r.at[row], w_ss.at[h], w_rs.at[row], h))
+
     pltpu.make_async_copy(dq_s.at[me], dq_r.at[me], loc.at[4]).wait()
     for peer in ctx_peers:
         ctx_arrived(dq_r, dq_ss, dq_rs, peer)
     for peer in ctx_peers:
         ctx_arrived(dkv_r, dkv_ss, dkv_rs, peer)
-    for peer in ctx_peers:
-        ctx_arrived(w_r, w_ss, w_rs, peer)
-    total = w_s[me].astype(jnp.float32)
-    for peer in ctx_peers:
-        total = total + w_r[peer].astype(jnp.float32)
-    w_out[...] = total
+    for a in orders[:-1]:
+        ctx_copy(w_r.at[a], w_r.at[a], w_ss.at[a], w_rs.at[a], pair).wait_recv()
+        w_out[...] += w_r[a].astype(jnp.float32)
     for peer in dp_peers:
         dp_arrived(mix_r, mix_ss, mix_rs, peer)
 
@@ -249,64 +304,35 @@
     for peer in ctx_peers:
         ctx_copy(attn_s.at[peer], attn_r.at[me], attn_ss.at[peer], attn_rs.at[me], peer).wait_send()
         ctx_copy(dq_s.at[peer], dq_r.at[me], dq_ss.at[peer], dq_rs.at[me], peer).wait_send()
-        ctx_copy(w_s.at[peer], w_r.at[me], w_ss.at[peer], w_rs.at[me], peer).wait_send()
 
 
 def shards(queries, keys, values, out_grad, chosen, proj):
     n = lax.axis_size("ctx")
     dn = lax.axis_size("dp")
-    me = lax.axis_index("ctx")
     tokens = queries.shape[1]
-    half_rows = tokens // 2
-    picked = chosen[0]
-    own_pick = lax.dynamic_index_in_dim(picked, me, 0, keepdims=False)
-    own_live = own_pick >= 0
-    first_pos = jnp.where(own_live, own_pick, 0) * BLOCK
-    local_row = jnp.where(
-        first_pos // half_rows == me,
-        first_pos % half_rows,
-        half_rows + first_pos % half_rows,
-    )
-    row_start = jnp.where(own_live, local_row, 0)
-
-    def take_rows(source):
-        slot_block = lax.dynamic_slice_in_dim(source[0], row_start, BLOCK, 0)
-        return jnp.where(own_live, slot_block, jnp.zeros((), source.dtype))
-
     dh = queries.shape[2] // n
     dc = proj.shape[1]
     slots = n * BLOCK
     width = 2 * BLOCK
     steps = n // 2
-
-    def by_head(rows):
-        return rows.reshape(BLOCK, n, dh).transpose(1, 0, 2)
-
-    qkv = jnp.stack([by_head(take_rows(x)) for x in (queries, keys, values)], axis=1)
-    g = take_rows(out_grad).reshape(BLOCK, dn, dc).transpose(1, 0, 2)
-
-    offsets = jnp.arange(BLOCK, dtype=jnp.int32)
-    live = picked >= 0
-    pos = (picked[:, None] * BLOCK + offsets[None, :])
-    key_pos = jnp.where(live[:, None], pos, FAR).reshape(slots)
-    query_pos = jnp.where(live[:, None], pos, -1).reshape(steps, 1, width)
-    key_pos = jnp.broadcast_to(key_pos[:, None], (slots, BLOCK))
-
     bf16, f32 = jnp.bfloat16, jnp.float32
     sem = pltpu.SemaphoreType.DMA
     vm = pltpu.VMEM
     blocks = (n, BLOCK, dh)
     scratch = [
+        vm((n, 3, BLOCK, dh), bf16), vm((dn, BLOCK, dc), bf16), vm((slots, BLOCK), jnp.int32),
         vm((n, 3, BLOCK, dh), bf16), vm((dn, BLOCK, dc), bf16), vm((n, dh, dc), bf16),
         vm((dn,) + blocks, bf16), vm((dn,) + blocks, bf16), vm(blocks, bf16), vm(blocks, bf16),
         vm(blocks, bf16), vm(blocks, bf16), vm((dn,) + blocks, bf16), vm((steps, dh, width), bf16),
         vm((steps, slots, width), bf16), vm((dh, slots), bf16), vm((dh, slots), bf16),
         vm(blocks, bf16), vm((n, 2, BLOCK, dh), bf16), vm((slots, dh), f32), vm((slots, dh), f32),
-        vm((n, dh, dc), bf16), vm((n, dh, dc), bf16), vm((dn, BLOCK, dc), bf16),
+        vm((n, dh, dc), bf16), vm((n // 2, dh, dc), bf16), vm((n // 2, dh, dc), bf16), vm((dn, BLOCK, dc), bf16),
     ]
     c, d = sem((n,)), sem((dn,))
-    sems = [c, c, d, d, c, c, c, d, d, c, c, c, c, d, d, c, c, c, c, c, c, d, d, sem((6,))]
-    dq, dkv, proj_grad, mixed = pl.pallas_call(
+    sems = [c, c, d, d, c, c, c, d, d, c, c, c, c, d, d, d, c, c, c, c, c, c, c, d, d, sem((6,))]
+    vmem = pl.BlockSpec(memory_space=pltpu.VMEM)
+    smem = pl.BlockSpec(memory_space=pltpu.SMEM)
+    dq, dkv, weight_grad, mixed = pl.pallas_call(
         functools.partial(kernel, n, dn, 1.0 / math.sqrt(dh)),
         out_shape=(
             jax.ShapeDtypeStruct(blocks, bf16),
@@ -314,30 +340,22 @@
             jax.ShapeDtypeStruct((dh, dc), f32),
             jax.ShapeDtypeStruct((dn, BLOCK, dc), bf16),
         ),
-        in_specs=[pl.BlockSpec(memory_space=pltpu.VMEM)] * 5,
+        in_specs=[smem] + [vmem] * 5,
         out_specs=[pl.BlockSpec(memory_space=pltpu.VMEM)] * 4,
         scratch_shapes=scratch + sems,
         compiler_params=pltpu.CompilerParams(
             collective_id=0, has_side_effects=True, vmem_limit_bytes=60 * 1024 * 1024),
-    )(qkv, g, proj, key_pos, query_pos)
-
-    count = tokens // BLOCK
-    here = (jnp.arange(count, dtype=jnp.int32) == row_start // BLOCK) & own_live
-
-    def place(rows):
-        out = jnp.where(here[:, None, None], rows[None], jnp.zeros((), rows.dtype))
-        return out.reshape(1, tokens, rows.shape[1])
-
-    def rows_of(parts):
-        return parts.transpose(1, 0, 2).reshape(BLOCK, parts.shape[0] * parts.shape[2])
-
-    return (
-        place(rows_of(mixed)),
-        place(rows_of(dq)),
-        place(rows_of(dkv[:, 0])),
-        place(rows_of(dkv[:, 1])),
-        proj_grad,
-    )
+    )(chosen, queries[0], keys[0], values[0], out_grad[0], proj)
+
+    wide = jax.ShapeDtypeStruct((tokens, dn * dc), bf16)
+    thin = jax.ShapeDtypeStruct((tokens, n * dh), bf16)
+    out, q_grad, k_grad, v_grad, proj_grad = pl.pallas_call(
+        functools.partial(place_kernel, n, dn, tokens // BLOCK),
+        out_shape=(wide, thin, thin, thin, jax.ShapeDtypeStruct((dh, dc), f32)),
+        in_specs=[smem] + [vmem] * 4,
+        out_specs=[vmem] * 5,
+    )(chosen, mixed, dq, dkv, weight_grad)
+    return out[None], q_grad[None], k_grad[None], v_grad[None], proj_grad
 
 
 def solution(mesh):

time: 119 us -> 91.1 us (0.77)
  local copies, waits for them, and re-layouts: 11.6 us -> 0 us
  Pallas kernels: 100 us -> 90.3 us
  other arithmetic: 4.23 us -> 0 us
  between operations: 2.27 us -> 0.64 us
    pallas_call x1, Pallas kernels: 100 us -> 87.1 us  [shards(): pl.pallas_call(functools.partial(kernel, n, dn, 1.0 / math.sqrt(dh)), out...]
    unnamed x19 -> x0, local copies, waits for them, and re-layouts: 3.78 us -> none
    pallas_call x0 -> x1, Pallas kernels: none -> 3.24 us  [shards(): pl.pallas_call(functools.partial(place_kernel, n, dn, tokens // BLOCK), o...]
    select_n x7 -> x0, other arithmetic: 3.21 us -> none  [the longest x2 2.43 us: place(): out = jnp.where(here[:, None, None], rows[None], jnp.zeros((), rows.dtype))]
    broadcast_in_dim x11 -> x0, local copies, waits for them, and re-layouts: 2.1 us -> none  [the longest x9 1.03 us: place(): out = jnp.where(here[:, None, None], rows[None], jnp.zeros((), rows.dtype))]
    dynamic_slice x5 -> x0, local copies, waits for them, and re-layouts: 1.93 us -> none  [the longest x4 1.35 us: take_rows(): slot_block = lax.dynamic_slice_in_dim(source[0], row_start, BLOCK, 0)]
    transpose x5 -> x0, local copies, waits for them, and re-layouts: 1.88 us -> none  [rows_of(): parts.transpose(1, 0, 2).reshape(BLOCK, parts.shape[0] * parts.shape[2])]
    select_n x4 -> x0, local copies, waits for them, and re-layouts: 1.55 us -> none  [take_rows(): return jnp.where(own_live, slot_block, jnp.zeros((), source.dtype))]
where the time goes in v2:
time: 91.1 us; the launch traced here: 91 us
  Pallas kernels  90.3 us (99%)
    pallas_call x1, Pallas kernels, shards(): pl.pallas_call(functools.partial(kernel, n, dn, 1.0 / math.sqrt(dh)), out...  87.1 us
    pallas_call x1, Pallas kernels, shards(): pl.pallas_call(functools.partial(place_kernel, n, dn, tokens // BLOCK), o...  3.24 us

profile of v2, /device:TPU:0, one launch (start us, length us, event | category | flops | bytes accessed | tf_op | source)
XLA Modules:
  0.0 91.0 jit_solution(14980326748128214459)
XLA Ops:
  0.6 87.1 %shard_map.101 = (bf16[8,128,128]{2,1,0:T(8,128)(2,1)}, bf16[8,2,128,128]{3,2,1,0:T(8,128)(2,1)}, f32[128,512]{1,0:T(8,128)}, bf16[4,128,512]{2,1,0:T(8,128)(2,1)}) custom-call(s32[1,8]{1,0:T(1,128)} %picked.3, bf16[256,1024]{1,0:T(8,128)(2,1)} %bitcast.9, bf16[256,1024]{1,0:T(8,128)(2,1)} %bitcast.10, bf16[256,1024]{1,0:T(8,128)(2,1)} %bitcast.11, ...), custom_call_target="tpu_custom_call" | custom-call | tf_op jit(solution)/shard_map/pallas_call | solution.py:335
  87.7 3.2 %shard_map.102 = (bf16[256,2048]{1,0:T(8,128)(2,1)}, bf16[256,1024]{1,0:T(8,128)(2,1)}, bf16[256,1024]{1,0:T(8,128)(2,1)}, bf16[256,1024]{1,0:T(8,128)(2,1)}, f32[128,512]{1,0:T(8,128)}) custom-call(s32[1,8]{1,0:T(1,128)} %picked.3, bf16[4,128,512]{2,1,0:T(8,128)(2,1)} %get-tuple-element.14.mix, bf16[8,128,128]{2,1,0:T(8,128)(2,1)} %get-tuple-element.15.dq, ...), custom_call_target="tpu_custom_call" | custom-call | tf_op jit(solution)/shard_map/pallas_call | solution.py:352

commit v3 on v2

--- a/solution.py
+++ b/solution.py
@@ -118,6 +118,12 @@
         for h in range(n):
             qkv[h, t] = chosen_rows(ref, h * dh, (h + 1) * dh)
     qkv_r[me] = qkv[me]
+
+    def send_qkv(peers):
+        for peer in peers:
+            go(ctx_copy(qkv.at[peer], qkv_r.at[me], qkv_ss.at[peer], qkv_rs.at[me], peer))
+
+    pair_far = [lax.rem(pair + 2 * s, n) for s in range(1, n // 2)]
     down = lax.broadcasted_iota(jnp.int32, (block, block), 0)
     for j in range(n):
         entry = picked[0, j]
@@ -130,46 +136,45 @@
     def dp_arrived(buf, ss, rs, peer):
         dp_copy(buf.at[peer], buf.at[peer], ss.at[peer], rs.at[peer], peer).wait_recv()
 
-    for peer in far:
-        ctx_arrived(proj_r, proj_ss, proj_rs, peer)
-        go(ctx_copy(proj_r.at[peer], proj_r.at[peer], fwd_ss.at[peer], proj_rs.at[peer], pair))
-    for peer in ctx_peers:
-        go(ctx_copy(qkv.at[peer], qkv_r.at[me], qkv_ss.at[peer], qkv_rs.at[me], peer))
-    for peer in [pair] + [lax.rem(pair + 2 * s, n) for s in range(1, n // 2)]:
-        ctx_arrived(proj_r, proj_ss, proj_rs, peer)
     for peer in dp_peers:
         dp_arrived(g_r, g_ss, g_rs, peer)
 
-    def part_step(j, carry):
-        heads = proj_r[pl.ds(2 * j, 2)].reshape(2 * dh, dc)
-        out = dot_nt(g_r[...].reshape(dn * block, dc), heads).astype(bf16)
-        agp_s[:, pl.ds(2 * j, 1)] = out[:, :dh].reshape(dn, 1, block, dh)
-        agp_s[:, pl.ds(2 * j + 1, 1)] = out[:, dh:].reshape(dn, 1, block, dh)
-        return carry
-
-    lax.fori_loop(0, steps, part_step, 0)
-    for peer in dp_peers:
-        go(dp_copy(agp_s.at[peer], agp_r.at[md], agp_ss.at[peer], agp_rs.at[md], peer))
+    def part(h):
+        out = dot_nt(g_r[...].reshape(dn * block, dc), proj_r[h]).astype(bf16)
+        agp_s[h] = out.reshape(dn, block, dh)
+        for peer in dp_peers:
+            go(dp_copy(agp_s.at[h, peer], agp_r.at[h, md], agp_ss.at[h, peer], agp_rs.at[h, md], peer))
+
+    def finish(h):
+        total = agp_s[h, md].astype(jnp.float32)
+        for peer in dp_peers:
+            dp_copy(agp_r.at[h, peer], agp_r.at[h, peer], agp_ss.at[h, peer], agp_rs.at[h, peer], peer).wait_recv()
+            total = total + agp_r[h, peer].astype(jnp.float32)
+        ag_s[h] = total.astype(bf16)
+        if h is me:
+            ag_r[me] = ag_s[me]
+        else:
+            go(ctx_copy(ag_s.at[h], ag_r.at[me], ag_ss.at[h], ag_rs.at[me], h))
+
+    heads = [me, pair] + far + pair_far
+    lag = 2
+    for k, h in enumerate(heads):
+        if k:
+            ctx_arrived(proj_r, proj_ss, proj_rs, h)
+        if 2 <= k < 2 + len(far):
+            go(ctx_copy(proj_r.at[h], proj_r.at[h], fwd_ss.at[h], proj_rs.at[h], pair))
+        part(h)
+        if k == 1 + len(far):
+            send_qkv(ctx_peers)
+        if k >= lag:
+            finish(heads[k - lag])
+    for h in heads[-lag:]:
+        finish(h)
 
     for peer in ctx_peers:
         ctx_arrived(qkv_r, qkv_ss, qkv_rs, peer)
     k_t[...] = transposed(qkv_r[:, 1].reshape(slots, dh))
     v_t[...] = transposed(qkv_r[:, 2].reshape(slots, dh))
-
-    for peer in dp_peers:
-        dp_arrived(agp_r, agp_ss, agp_rs, peer)
-
-    def sum_step(h, carry):
-        total = agp_s[md, h].astype(jnp.float32)
-        for peer in dp_peers:
-            total = total + agp_r[peer, h].astype(jnp.float32)
-        ag_s[h] = total.astype(bf16)
-        return carry
-
-    lax.fori_loop(0, n, sum_step, 0)
-    for peer in ctx_peers:
-        go(ctx_copy(ag_s.at[peer], ag_r.at[me], ag_ss.at[peer], ag_rs.at[me], peer))
-    ag_r[me] = ag_s[me]
 
     def send_pair(i, src, dst, ss, rs, own_sem):
         for half in range(2):
@@ -322,14 +327,15 @@
     scratch = [
         vm((n, 3, BLOCK, dh), bf16), vm((dn, BLOCK, dc), bf16), vm((slots, BLOCK), jnp.int32),
         vm((n, 3, BLOCK, dh), bf16), vm((dn, BLOCK, dc), bf16), vm((n, dh, dc), bf16),
-        vm((dn,) + blocks, bf16), vm((dn,) + blocks, bf16), vm(blocks, bf16), vm(blocks, bf16),
+        vm((n, dn, BLOCK, dh), bf16), vm((n, dn, BLOCK, dh), bf16), vm(blocks, bf16), vm(blocks, bf16),
         vm(blocks, bf16), vm(blocks, bf16), vm((dn,) + blocks, bf16), vm((steps, dh, width), bf16),
         vm((steps, slots, width), bf16), vm((dh, slots), bf16), vm((dh, slots), bf16),
         vm(blocks, bf16), vm((n, 2, BLOCK, dh), bf16), vm((slots, dh), f32), vm((slots, dh), f32),
         vm((n, dh, dc), bf16), vm((n // 2, dh, dc), bf16), vm((n // 2, dh, dc), bf16), vm((dn, BLOCK, dc), bf16),
     ]
     c, d = sem((n,)), sem((dn,))
-    sems = [c, c, d, d, c, c, c, d, d, c, c, c, c, d, d, d, c, c, c, c, c, c, c, d, d, sem((6,))]
+    e = sem((n, dn))
+    sems = [c, c, d, d, c, c, c, e, e, c, c, c, c, d, d, d, c, c, c, c, c, c, c, d, d, sem((6,))]
     vmem = pl.BlockSpec(memory_space=pltpu.VMEM)
     smem = pl.BlockSpec(memory_space=pltpu.SMEM)
     dq, dkv, weight_grad, mixed = pl.pallas_call(

time: 91.1 us -> 87.8 us (0.964)
  Pallas kernels: 90.3 us -> 87 us
    pallas_call x1, Pallas kernels: 87.1 us -> 83.7 us  [shards(): pl.pallas_call(functools.partial(kernel, n, dn, 1.0 / math.sqrt(dh)), out...]
where the time goes in v3:
time: 87.8 us; the launch traced here: 87.6 us
  Pallas kernels  87 us (99%)
    pallas_call x1, Pallas kernels, shards(): pl.pallas_call(functools.partial(kernel, n, dn, 1.0 / math.sqrt(dh)), out...  83.7 us
    pallas_call x1, Pallas kernels, shards(): pl.pallas_call(functools.partial(place_kernel, n, dn, tokens // BLOCK), o...  3.24 us

profile of v3, /device:TPU:0, one launch (start us, length us, event | category | flops | bytes accessed | tf_op | source)
XLA Modules:
  0.0 87.6 jit_solution(169175872633799859)
XLA Ops:
  0.6 83.7 %shard_map.101 = (bf16[8,128,128]{2,1,0:T(8,128)(2,1)}, bf16[8,2,128,128]{3,2,1,0:T(8,128)(2,1)}, f32[128,512]{1,0:T(8,128)}, bf16[4,128,512]{2,1,0:T(8,128)(2,1)}) custom-call(s32[1,8]{1,0:T(1,128)} %picked.3, bf16[256,1024]{1,0:T(8,128)(2,1)} %bitcast.9, bf16[256,1024]{1,0:T(8,128)(2,1)} %bitcast.10, bf16[256,1024]{1,0:T(8,128)(2,1)} %bitcast.11, ...), custom_call_target="tpu_custom_call" | custom-call | tf_op jit(solution)/shard_map/pallas_call | solution.py:341
  84.4 3.2 %shard_map.102 = (bf16[256,2048]{1,0:T(8,128)(2,1)}, bf16[256,1024]{1,0:T(8,128)(2,1)}, bf16[256,1024]{1,0:T(8,128)(2,1)}, bf16[256,1024]{1,0:T(8,128)(2,1)}, f32[128,512]{1,0:T(8,128)}) custom-call(s32[1,8]{1,0:T(1,128)} %picked.3, bf16[4,128,512]{2,1,0:T(8,128)(2,1)} %get-tuple-element.14.mix, bf16[8,128,128]{2,1,0:T(8,128)(2,1)} %get-tuple-element.15.dq, ...), custom_call_target="tpu_custom_call" | custom-call | tf_op jit(solution)/shard_map/pallas_call | solution.py:358
